TPU v7x, 32 devices: a whole 2x2x4 slice. The times are simulated.
32 devices in a mesh: seq: 16 (over z, y, x), mp: 2 (over core).
Axes of the slice: x: 2, y: 2, z: 4, core: 2. Of those that a mesh axis runs over, the one named last changes fastest.
Arguments:
- layer_input: bfloat16 [128, 8192], P('seq'), may hold values from -6 to 6
- w_query: bfloat16 [8192, 8192], P('seq', 'mp'), may hold values from -0.0625 to 0.0625
- w_key: bfloat16 [8192, 1024], P('seq', 'mp'), may hold values from -0.1875 to 0.1875
- w_value: bfloat16 [8192, 1024], P('seq', 'mp'), may hold values from -0.0625 to 0.0625
- w_out: bfloat16 [8192, 8192], P('mp', 'seq'), may hold values from -0.0625 to 0.0625
- kv_cache: bfloat16 [2, 32, 4096, 1024], P(None, None, 'seq', 'mp'), may hold values from -180 to 180, as said below
- cache_len: int32 [32], replicated, may hold values from 1 to 4096, as said below
Outputs:
- attn_out: bfloat16 [128, 8192], P('mp', 'seq')
Inputs may be any that keep to these rules, and one draw needn't show every extreme that they name: kv_cache entries at positions at or beyond a request's cache_len are never read. `cache_len`: exactly 4096 for at least one request.
All inputs are finite; a program needn't handle non-finite values.
Results may differ from a plain program's by a relative error of at most 0.012.
The roundings to bfloat16 on the way count: a program that leaves them out, or rounds other values in their place, can miss the bound.
Values may be sent and summed in bfloat16 or wider, within the bound.
A program may use at most 192 MiB of HBM per device.

v0:
```python
import math
import jax
import jax.numpy as jnp
from jax import lax
from jax.sharding import PartitionSpec as P

HD = 128
NEG_FILL = -1e30


def inverse_freq():
    index = jnp.arange(HD // 2, dtype=jnp.float32)
    base_freq = jnp.exp(-(2.0 * index / HD) * math.log(500000.0))
    wavelength = 2.0 * math.pi / base_freq
    smooth = jnp.clip((8192.0 / wavelength - 1.0) / 3.0, 0.0, 1.0)
    return (1.0 - smooth) * base_freq / 8.0 + smooth * base_freq


def rotate(values, positions):
    angles = positions.astype(jnp.float32)[..., None] * inverse_freq()
    cosine = jnp.cos(angles)
    sines = jnp.sin(angles)
    half_width = HD // 2
    first_half = values[..., :half_width]
    second_half = values[..., half_width:]
    return jnp.concatenate(
        [first_half * cosine - second_half * sines, second_half * cosine + first_half * sines],
        axis=-1,
    )


def shards(layer_input, w_query, w_key, w_value, w_out, kv_cache, cache_len):
    widened = layer_input.astype(jnp.float32)
    normed = (
        widened * lax.rsqrt(jnp.mean(widened * widened, axis=-1, keepdims=True) + 1e-05)
    ).astype(jnp.bfloat16)
    gathered = lax.all_to_all(normed, "seq", split_axis=1, concat_axis=0, tiled=True)
    partial_query = jnp.dot(gathered, w_query, preferred_element_type=jnp.float32)
    partial_key = jnp.dot(gathered, w_key, preferred_element_type=jnp.float32)
    partial_value = jnp.dot(gathered, w_value, preferred_element_type=jnp.float32)
    row_count = gathered.shape[0]
    request_count = cache_len.shape[0]
    decode_count = row_count // request_count
    heads_here = partial_query.shape[1] // HD
    kv_here = partial_key.shape[1] // HD
    group_size = heads_here // kv_here
    score_scale = 1.0 / math.sqrt(HD)
    highest = lax.Precision.HIGHEST
    query_all, key_all, value_all = lax.psum((partial_query, partial_key, partial_value), "seq")
    positions = (cache_len[:, None] + jnp.arange(decode_count, dtype=jnp.int32)[None, :]).reshape(
        row_count
    )
    queries = rotate(query_all.reshape(row_count, heads_here, HD), positions[:, None]).astype(
        jnp.bfloat16
    )
    keys_new = rotate(key_all.reshape(row_count, kv_here, HD), positions[:, None]).astype(
        jnp.bfloat16
    )
    values_new = value_all.astype(jnp.bfloat16)
    queries = queries.reshape(request_count, decode_count, kv_here, group_size, HD)
    keys_new = keys_new.reshape(request_count, decode_count, kv_here, HD)
    values_new = values_new.reshape(request_count, decode_count, kv_here, HD)
    block_size = kv_cache.shape[2]
    cache_keys = kv_cache[0].reshape(request_count, block_size, kv_here, HD)
    cache_values = kv_cache[1].reshape(request_count, block_size, kv_here, HD).astype(jnp.float32)
    first_slot = lax.axis_index("seq") * block_size
    slot_index = first_slot + jnp.arange(block_size, dtype=jnp.int32)
    active_slot = (slot_index[None, :] < cache_len[:, None])[:, None, None, None, :]
    causal = (jnp.arange(decode_count)[:, None] >= jnp.arange(decode_count)[None, :])[
        None, None, None
    ]
    old_scores = (
        jnp.einsum("rtkgd,rpkd->rkgtp", queries, cache_keys, preferred_element_type=jnp.float32)
        * score_scale
    )
    old_scores = jnp.where(active_slot, old_scores, NEG_FILL)
    old_top = jnp.max(old_scores, axis=-1)
    new_scores = (
        jnp.einsum("rtkgd,rukd->rkgtu", queries, keys_new, preferred_element_type=jnp.float32)
        * score_scale
    )
    new_scores = jnp.where(causal, new_scores, NEG_FILL)
    new_top = jnp.max(new_scores, axis=-1)
    row_top = lax.pmax(jnp.maximum(old_top, new_top), "seq")
    old_weights = jnp.where(active_slot, jnp.exp(old_scores - row_top[..., None]), 0.0)
    old_total, old_pooled = lax.psum(
        (
            jnp.sum(old_weights, axis=-1),
            jnp.einsum("rkgtp,rpkd->rkgtd", old_weights, cache_values, precision=highest),
        ),
        "seq",
    )
    new_weights = jnp.where(causal, jnp.exp(new_scores - row_top[..., None]), 0.0)
    denominator = old_total + jnp.sum(new_weights, axis=-1)
    pooled = old_pooled + jnp.einsum(
        "rkgtu,rukd->rkgtd", new_weights, values_new.astype(jnp.float32), precision=highest
    )
    attended = (
        (pooled / denominator[..., None])
        .transpose(0, 3, 1, 2, 4)
        .reshape(row_count, heads_here * HD)
        .astype(jnp.bfloat16)
    )
    return lax.psum_scatter(
        jnp.dot(attended, w_out, preferred_element_type=jnp.float32).astype(jnp.bfloat16),
        "mp",
        scatter_dimension=0,
        tiled=True,
    )


def solution(mesh):
    return jax.shard_map(
        shards,
        mesh=mesh,
        in_specs=(
            P("seq", None),
            P("seq", "mp"),
            P("seq", "mp"),
            P("seq", "mp"),
            P("mp", "seq"),
            P(None, None, "seq", "mp"),
            P(),
        ),
        out_specs=P("mp", "seq"),
        check_vma=False,
    )
```

profile of v0, /device:TPU:0, one launch (start us, length us, event | category | flops | bytes accessed | tf_op | source)
XLA Modules:
  0.0 416.0 jit_solution(5943476113532040646)
XLA Ops:
  6.5 1.1 fusion.21
  7.7 1.6 fusion.22
  9.3 8.3 %all-to-all-start = ((bf16[8,16,512]{2,0,1:T(8,128)(2,1)}), bf16[8,16,512]{2,0,1:T(8,128)(2,1)S(1)}, u32[]{:S(2)}, u32[]{:S(2)}) async-start(bf16[8,16,512]{2,0,1:T(8,128)(2,1)} %bitcast), calls=%async_computation | async-start | bytes 262144 | tf_op jit(solution)/shard_map/all_to_all | solution.py:37
  17.7 7.7 %all-to-all-done = bf16[8,16,512]{2,0,1:T(8,128)(2,1)S(1)} async-done(((bf16[8,16,512]{2,0,1:T(8,128)(2,1)}), bf16[8,16,512]{2,0,1:T(8,128)(2,1)S(1)}, u32[]{:S(2)}, u32[]{:S(2)}) %all-to-all-start) | async-done | bytes 131104 | tf_op jit(solution)/shard_map/all_to_all | solution.py:37
  25.4 2.9 convolution_bitcast_fusion
  28.4 1.7 copy.37
  30.2 0.7 copy.53
  31.0 11.8 %fusion.33 = (bf16[1,32,256,512]{3,2,1,0:T(8,128)(2,1)}, bf16[1,32,256,512]{3,2,1,0:T(8,128)(2,1)}) fusion(bf16[2,32,256,512]{3,2,1,0:T(8,128)(2,1)} %param.12), kind=kLoop, calls=%fused_computation.58 | loop fusion | bytes 33554432 | tf_op jit(solution)/shard_map/slice | solution.py:64
  42.8 12.0 %copy.35 = bf16[1,32,256,512]{2,3,1,0:T(8,128)(2,1)} copy(bf16[1,32,256,512]{3,2,1,0:T(8,128)(2,1)} %get-tuple-element.10) | data formatting | bytes 16777216
  54.8 11.9 %copy.34 = bf16[1,32,256,512]{2,3,1,0:T(8,128)(2,1)} copy(bf16[1,32,256,512]{3,2,1,0:T(8,128)(2,1)} %get-tuple-element.9) | data formatting | bytes 16777216
  67.4 92.3 %all-reduce.8.cloned.1.call-done = (f32[128,32,128]{2,1,0:T(8,128)}, f32[128,4,128]{2,0,1:T(8,128)}) async-done(((f32[128,32,128]{2,1,0:T(8,128)}, f32[128,4,128]{2,0,1:T(8,128)}), (f32[128,32,128]{2,1,0:T(8,128)}, f32[128,4,128]{2,0,1:T(8,128)})) %all-reduce.8.cloned.1.call-update) | async-done | bytes 2359312 | tf_op jit(solution)/shard_map/psum | solution.py:49
  159.6 3.1 subtract_convert_fusion
  162.9 7.1 %bitcast_reduce_fusion = (f32[32,4,8,4]{2,3,1,0:T(4,128)S(1)}, f32[32,4,4,8,256]{4,3,2,1,0:T(8,128)}) fusion(pred[32,256]{1,0:T(8,128)(4,1)S(1)} %broadcast_compare_fusion, bf16[32,256,4,128,1]{1,3,4,2,0:T(8,128)(2,1)} %bitcast.63, bf16[32,4,4,8,64]{4,3,2,1,0:T(8,128)(2,1)S(1)} %bitcast.67, bf16[32,4,4,8,64]{4,3,2,1,0:T(8,128)(2,1)S(1)} %bitcast.65), kind=kOutput, calls=%fused_computation.1 | convolution fusion | flops 273674240 | bytes 13656064 | tf_op jit(solution)/shard_map/rtkgd,rpkd->rkgtp/dot_general | solution.py:73
  170.0 5.0 %fusion.34 = (f32[32,4,8,4]{2,3,1,0:T(4,128)S(1)}, f32[32,4,8,4,4]{2,4,3,1,0:T(4,128)S(1)}) fusion(pred[4,4]{1,0:T(4,128)(4,1)S(1)} %iota_compare_fusion, bf16[32,4,4,64]{3,1,0,2:T(4,128)(2,1)S(1)} %bitcast.71, bf16[32,4,4,64]{3,1,0,2:T(4,128)(2,1)S(1)} %bitcast.70, bf16[32,4,4,8,64]{4,3,2,1,0:T(8,128)(2,1)S(1)} %bitcast.68, ...), kind=kOutput, calls=%fused_computation.59 | convolution fusion | flops 6598656 | bytes 1261584 | tf_op jit(solution)/shard_map/rtkgd,rukd->rkgtu/dot_general | solution.py:79
  175.1 78.2 %pmax.7 = f32[32,4,8,4]{2,3,1,0:T(4,128)S(1)} all-reduce(f32[32,4,8,4]{2,3,1,0:T(4,128)S(1)} %max.14), channel_id=1, replica_groups=mesh['seq'=16,'mp'=2] {'seq'}, use_global_device_ids=true, to_apply=%region_5.6 | all-reduce | flops 4096 | bytes 32768 | tf_op jit(solution)/shard_map/pmax | solution.py:84
  253.3 14.2 %fusion.3 = f32[32,4,8,4,128]{4,2,3,1,0:T(8,128)} fusion(bf16[32,256,4,128,1]{1,3,4,2,0:T(8,128)(2,1)} %bitcast.62, f32[32,4,4,8,256]{4,3,2,1,0:T(8,128)} %get-tuple-element.18, f32[32,4,8,4]{2,3,1,0:T(4,128)S(1)} %pmax.7, pred[32,256]{1,0:T(8,128)(4,1)S(1)} %broadcast_compare_fusion), kind=kOutput, calls=%fused_computation.6 | convolution fusion | flops 1614807040 | bytes 14704640 | tf_op jit(solution)/shard_map/rkgtp,rpkd->rkgtd/dot_general | solution.py:89
  267.8 3.6 fusion.2
  271.4 81.3 %all-reduce.9 = (f32[32,4,8,4]{2,3,1,0:T(4,128)S(1)}, bf16[128,512]{1,0:T(8,128)(2,1)S(1)}) all-reduce(f32[32,4,8,4]{2,3,1,0:T(4,128)S(1)} %fusion.2, f32[128,512]{1,0:T(8,128)S(1)} %fusion.25), channel_id=1, replica_groups=mesh['seq'=16,'mp'=2] {'seq'}, use_global_device_ids=true, to_apply=%region_9.10 | all-reduce | flops 69632 | bytes 425984 | tf_op jit(solution)/shard_map/psum | solution.py:86
  352.7 1.0 fusion.17
  353.8 40.5 %all-reduce.6.cloned.1.call-done = f32[32,4,8,4,128]{4,2,3,1,0:T(8,128)} async-done(((f32[32,4,8,4,128]{4,2,3,1,0:T(8,128)}), f32[32,4,8,4,128]{4,2,3,1,0:T(8,128)}) %all-reduce.6.cloned.1.call-update) | async-done | bytes 2097168 | tf_op jit(solution)/shard_map/psum | solution.py:86
  394.4 3.8 fusion.11
  398.4 0.5 convert_element_type.47
  398.9 3.5 convolution_convert_fusion
  402.5 7.0 %reduce-scatter.2.cloned.1.call-done = bf16[64,512]{1,0:T(8,128)(2,1)} async-done(((bf16[128,512]{1,0:T(8,128)(2,1)}), bf16[64,512]{1,0:T(8,128)(2,1)}) %reduce-scatter.2.cloned.1.call-update) | async-done | bytes 65552 | tf_op jit(solution)/shard_map/reduce_scatter | solution.py:104
  (31 shorter events, 1.8 us)
Async XLA Ops:
  6.5 23.5 %copy-start = (bf16[512,512]{1,0:T(8,128)(2,1)S(1)}, bf16[512,512]{1,0:T(8,128)(2,1)}, u32[]{:S(2)}) copy-start(bf16[512,512]{1,0:T(8,128)(2,1)} %param.9) | copy-start | bytes 1572868
  9.3 16.1 %all-to-all-start = ((bf16[8,16,512]{2,0,1:T(8,128)(2,1)}), bf16[8,16,512]{2,0,1:T(8,128)(2,1)S(1)}, u32[]{:S(2)}, u32[]{:S(2)}) async-start(bf16[8,16,512]{2,0,1:T(8,128)(2,1)} %bitcast), calls=%async_computation | async-start | bytes 262144 | tf_op jit(solution)/shard_map/all_to_all | solution.py:37
  17.6 142.0 %all-reduce.8.cloned.1.call-start = ((), (), s32[]{:S(2)}) async-start(), calls=%async_computation.4 | async-start | bytes 4718592 | tf_op jit(solution)/shard_map/psum | solution.py:49
  31.0 363.4 %all-reduce.6.cloned.1.call-start = ((), (), s32[]{:S(2)}) async-start(), calls=%async_computation.2 | async-start | bytes 4194304 | tf_op jit(solution)/shard_map/psum | solution.py:86
  54.8 11.9 %copy-start.4 = (s32[32]{0:T(128)S(1)}, s32[32]{0:T(128)}, u32[]{:S(2)}) copy-start(s32[32]{0:T(128)} %param.13) | copy-start | bytes 388
  159.6 3.1 copy-start.2
  253.3 14.3 %copy-start.3 = (bf16[512,512]{1,0:T(8,128)(2,1)S(1)}, bf16[512,512]{1,0:T(8,128)(2,1)}, u32[]{:S(2)}) copy-start(bf16[512,512]{1,0:T(8,128)(2,1)} %param.10) | copy-start | bytes 1572868
  267.5 142.0 %reduce-scatter.2.cloned.1.call-start = ((), (), s32[]{:S(2)}) async-start(), calls=%async_computation.3 | async-start | bytes 196608 | tf_op jit(solution)/shard_map/reduce_scatter | solution.py:104
  398.2 11.3 %copy-start.1 = (bf16[512,512]{1,0:T(8,128)(2,1)S(1)}, bf16[512,512]{1,0:T(8,128)(2,1)}, u32[]{:S(2)}) copy-start(bf16[512,512]{1,0:T(8,128)(2,1)} %param.9) | copy-start | bytes 1572868
Sparse Core Ops, SparseCore 0:
  31.1 128.4 all-reduce.7
  267.6 126.7 all-reduce.5
  402.6 6.8 reduce-scatter.1
where the time goes:
time: 417 us; the launch traced here: 416 us
  blocking collectives  159 us (38%)
  waiting for transfers between devices  148 us (35%)
  local copies, waits for them, and re-layouts  38.9 us (9%)
  matrix products  37.1 us (9%)
  between operations  13.3 us (3%)
  other arithmetic  11.3 us (3%)
  starting transfers between devices  8.44 us (2%)
    psum x1, waiting for transfers between devices, shards(): lax.psum((partial_query, partial_key, partial_value), 'seq')  92.3 us
    psum x1, blocking collectives, shards(): lax.psum((jnp.sum(old_weights, axis=-1), jnp.einsum('rkgtp,rpkd->rkgtd',...  81.3 us
    pmax x1, blocking collectives, shards(): row_top = lax.pmax(jnp.maximum(old_top, new_top), 'seq')  78.2 us
    psum x1, waiting for transfers between devices, shards(): lax.psum((jnp.sum(old_weights, axis=-1), jnp.einsum('rkgtp,rpkd->rkgtd',...  40.5 us
    unnamed x13, local copies, waits for them, and re-layouts  25.6 us
    dot_general x1, matrix products, shards(): jnp.einsum('rkgtp,rpkd->rkgtd', old_weights, cache_values, precision=high...  14.2 us
    slice x1, local copies, waits for them, and re-layouts, shards(): cache_keys = kv_cache[0].reshape(request_count, block_size, kv_here, HD)  11.8 us
  transfers between devices with their start and end apart: 4, of which 4 were waited for; matrix products, arithmetic and copies ran while one was open for 10% of the time, Pallas kernels for 0%

commit v1 on v0

--- a/solution.py
+++ b/solution.py
@@ -34,7 +34,9 @@
     normed = (
         widened * lax.rsqrt(jnp.mean(widened * widened, axis=-1, keepdims=True) + 1e-05)
     ).astype(jnp.bfloat16)
-    gathered = lax.all_to_all(normed, "seq", split_axis=1, concat_axis=0, tiled=True)
+    shards_2 = jnp.split(normed, lax.axis_size("seq"), axis=1)
+    incoming = lax.all_to_all(jnp.stack(shards_2), "seq", 0, 0)
+    gathered = jnp.concatenate(incoming, axis=0)
     partial_query = jnp.dot(gathered, w_query, preferred_element_type=jnp.float32)
     partial_key = jnp.dot(gathered, w_key, preferred_element_type=jnp.float32)
     partial_value = jnp.dot(gathered, w_value, preferred_element_type=jnp.float32)

time: 417 us -> 426 us (1.022)
  local copies, waits for them, and re-layouts: 38.9 us -> 48.4 us
    unnamed x13 -> x28, local copies, waits for them, and re-layouts: 25.6 us -> 34.5 us
where the time goes in v1:
time: 426 us; the launch traced here: 425 us
  blocking collectives  159 us (37%)
  waiting for transfers between devices  148 us (35%)
  local copies, waits for them, and re-layouts  48.4 us (11%)
  matrix products  37 us (9%)
  between operations  13.3 us (3%)
  other arithmetic  10.6 us (2%)
  starting transfers between devices  8.44 us (2%)
    psum x1, waiting for transfers between devices, shards(): lax.psum((partial_query, partial_key, partial_value), 'seq')  92.3 us
    psum x1, blocking collectives, shards(): lax.psum((jnp.sum(old_weights, axis=-1), jnp.einsum('rkgtp,rpkd->rkgtd',...  81.2 us
    pmax x1, blocking collectives, shards(): row_top = lax.pmax(jnp.maximum(old_top, new_top), 'seq')  78.2 us
    psum x1, waiting for transfers between devices, shards(): lax.psum((jnp.sum(old_weights, axis=-1), jnp.einsum('rkgtp,rpkd->rkgtd',...  40.7 us
    unnamed x28, local copies, waits for them, and re-layouts  34.5 us
    dot_general x1, matrix products, shards(): jnp.einsum('rkgtp,rpkd->rkgtd', old_weights, cache_values, precision=high...  14.2 us
    slice x1, local copies, waits for them, and re-layouts, shards(): cache_keys = kv_cache[0].reshape(request_count, block_size, kv_here, HD)  11.8 us
  transfers between devices with their start and end apart: 4, of which 4 were waited for; matrix products, arithmetic and copies ran while one was open for 10% of the time, Pallas kernels for 0%

profile of v1, /device:TPU:0, one launch (start us, length us, event | category | flops | bytes accessed | tf_op | source)
XLA Modules:
  0.0 425.0 jit_solution(13864793072364935634)
XLA Ops:
  6.5 1.1 fusion.21
  7.7 1.0 fusion.22
  17.0 0.6 constant_dynamic-update-slice_fusion.1
  18.2 8.3 %all-to-all-start = ((bf16[16,8,512]{2,1,0:T(8,128)(2,1)}), bf16[16,8,512]{2,1,0:T(8,128)(2,1)S(1)}, u32[]{:S(2)}, u32[]{:S(2)}) async-start(bf16[16,8,512]{2,1,0:T(8,128)(2,1)} %constant_dynamic-update-slice_fusion), calls=%async_computation | async-start | bytes 262144 | tf_op jit(solution)/shard_map/all_to_all | solution.py:38
  26.6 7.7 %all-to-all-done = bf16[16,8,512]{2,1,0:T(8,128)(2,1)S(1)} async-done(((bf16[16,8,512]{2,1,0:T(8,128)(2,1)}), bf16[16,8,512]{2,1,0:T(8,128)(2,1)S(1)}, u32[]{:S(2)}, u32[]{:S(2)}) %all-to-all-start) | async-done | bytes 131104 | tf_op jit(solution)/shard_map/all_to_all | solution.py:38
  34.3 2.9 convolution_bitcast_fusion
  37.2 1.7 copy.37
  39.1 0.7 copy.53
  39.9 11.8 %fusion.33 = (bf16[1,32,256,512]{3,2,1,0:T(8,128)(2,1)}, bf16[1,32,256,512]{3,2,1,0:T(8,128)(2,1)}) fusion(bf16[2,32,256,512]{3,2,1,0:T(8,128)(2,1)} %param.12), kind=kLoop, calls=%fused_computation.90 | loop fusion | bytes 33554432 | tf_op jit(solution)/shard_map/slice | solution.py:66
  51.7 12.0 %copy.35 = bf16[1,32,256,512]{2,3,1,0:T(8,128)(2,1)} copy(bf16[1,32,256,512]{3,2,1,0:T(8,128)(2,1)} %get-tuple-element.10) | data formatting | bytes 16777216
  63.7 11.9 %copy.34 = bf16[1,32,256,512]{2,3,1,0:T(8,128)(2,1)} copy(bf16[1,32,256,512]{3,2,1,0:T(8,128)(2,1)} %get-tuple-element.9) | data formatting | bytes 16777216
  76.2 92.3 %all-reduce.8.cloned.1.call-done = (f32[128,32,128]{2,1,0:T(8,128)}, f32[128,4,128]{2,0,1:T(8,128)}) async-done(((f32[128,32,128]{2,1,0:T(8,128)}, f32[128,4,128]{2,0,1:T(8,128)}), (f32[128,32,128]{2,1,0:T(8,128)}, f32[128,4,128]{2,0,1:T(8,128)})) %all-reduce.8.cloned.1.call-update) | async-done | bytes 2359312 | tf_op jit(solution)/shard_map/psum | solution.py:51
  168.5 3.1 subtract_convert_fusion
  171.7 7.1 %bitcast_reduce_fusion = (f32[32,4,8,4]{2,3,1,0:T(4,128)S(1)}, f32[32,4,4,8,256]{4,3,2,1,0:T(8,128)}) fusion(pred[32,256]{1,0:T(8,128)(4,1)S(1)} %broadcast_compare_fusion, bf16[32,256,4,128,1]{1,3,4,2,0:T(8,128)(2,1)} %bitcast.124, bf16[32,4,4,8,64]{4,3,2,1,0:T(8,128)(2,1)S(1)} %bitcast.128, bf16[32,4,4,8,64]{4,3,2,1,0:T(8,128)(2,1)S(1)} %bitcast.126), kind=kOutput, calls=%fused_computation.1 | convolution fusion | flops 273674240 | bytes 13656064 | tf_op jit(solution)/shard_map/rtkgd,rpkd->rkgtp/dot_general | solution.py:75
  178.9 5.0 %fusion.34 = (f32[32,4,8,4]{2,3,1,0:T(4,128)S(1)}, f32[32,4,8,4,4]{2,4,3,1,0:T(4,128)S(1)}) fusion(pred[4,4]{1,0:T(4,128)(4,1)S(1)} %iota_compare_fusion, bf16[32,4,4,64]{3,1,0,2:T(4,128)(2,1)S(1)} %bitcast.132, bf16[32,4,4,64]{3,1,0,2:T(4,128)(2,1)S(1)} %bitcast.131, bf16[32,4,4,8,64]{4,3,2,1,0:T(8,128)(2,1)S(1)} %bitcast.129, ...), kind=kOutput, calls=%fused_computation.91 | convolution fusion | flops 6598656 | bytes 1261584 | tf_op jit(solution)/shard_map/rtkgd,rukd->rkgtu/dot_general | solution.py:81
  184.0 78.2 %pmax.7 = f32[32,4,8,4]{2,3,1,0:T(4,128)S(1)} all-reduce(f32[32,4,8,4]{2,3,1,0:T(4,128)S(1)} %max.14), channel_id=1, replica_groups=mesh['seq'=16,'mp'=2] {'seq'}, use_global_device_ids=true, to_apply=%region_5.6 | all-reduce | flops 4096 | bytes 32768 | tf_op jit(solution)/shard_map/pmax | solution.py:86
  262.2 14.2 %fusion.3 = f32[32,4,8,4,128]{4,2,3,1,0:T(8,128)} fusion(bf16[32,256,4,128,1]{1,3,4,2,0:T(8,128)(2,1)} %bitcast.123, f32[32,4,4,8,256]{4,3,2,1,0:T(8,128)} %get-tuple-element.18, f32[32,4,8,4]{2,3,1,0:T(4,128)S(1)} %pmax.7, pred[32,256]{1,0:T(8,128)(4,1)S(1)} %broadcast_compare_fusion), kind=kOutput, calls=%fused_computation.6 | convolution fusion | flops 1614807040 | bytes 14704640 | tf_op jit(solution)/shard_map/rkgtp,rpkd->rkgtd/dot_general | solution.py:91
  276.7 3.6 fusion.2
  280.3 81.2 %all-reduce.9 = (f32[32,4,8,4]{2,3,1,0:T(4,128)S(1)}, bf16[128,512]{1,0:T(8,128)(2,1)S(1)}) all-reduce(f32[32,4,8,4]{2,3,1,0:T(4,128)S(1)} %fusion.2, f32[128,512]{1,0:T(8,128)S(1)} %fusion.25), channel_id=1, replica_groups=mesh['seq'=16,'mp'=2] {'seq'}, use_global_device_ids=true, to_apply=%region_9.10 | all-reduce | flops 69632 | bytes 425984 | tf_op jit(solution)/shard_map/psum | solution.py:88
  361.5 1.0 fusion.17
  362.6 40.7 %all-reduce.6.cloned.1.call-done = f32[32,4,8,4,128]{4,2,3,1,0:T(8,128)} async-done(((f32[32,4,8,4,128]{4,2,3,1,0:T(8,128)}), f32[32,4,8,4,128]{4,2,3,1,0:T(8,128)}) %all-reduce.6.cloned.1.call-update) | async-done | bytes 2097168 | tf_op jit(solution)/shard_map/psum | solution.py:88
  403.3 3.8 fusion.11
  407.9 3.6 convolution_convert_fusion
  411.4 7.0 %reduce-scatter.2.cloned.1.call-done = bf16[64,512]{1,0:T(8,128)(2,1)} async-done(((bf16[128,512]{1,0:T(8,128)(2,1)}), bf16[64,512]{1,0:T(8,128)(2,1)}) %reduce-scatter.2.cloned.1.call-update) | async-done | bytes 65552 | tf_op jit(solution)/shard_map/reduce_scatter | solution.py:106
  (47 shorter events, 11.2 us)
Async XLA Ops:
  6.5 32.4 %copy-start = (bf16[512,512]{1,0:T(8,128)(2,1)S(1)}, bf16[512,512]{1,0:T(8,128)(2,1)}, u32[]{:S(2)}) copy-start(bf16[512,512]{1,0:T(8,128)(2,1)} %param.9) | copy-start | bytes 1572868
  18.2 16.1 %all-to-all-start = ((bf16[16,8,512]{2,1,0:T(8,128)(2,1)}), bf16[16,8,512]{2,1,0:T(8,128)(2,1)S(1)}, u32[]{:S(2)}, u32[]{:S(2)}) async-start(bf16[16,8,512]{2,1,0:T(8,128)(2,1)} %constant_dynamic-update-slice_fusion), calls=%async_computation | async-start | bytes 262144 | tf_op jit(solution)/shard_map/all_to_all | solution.py:38
  26.5 142.0 %all-reduce.8.cloned.1.call-start = ((), (), s32[]{:S(2)}) async-start(), calls=%async_computation.4 | async-start | bytes 4718592 | tf_op jit(solution)/shard_map/psum | solution.py:51
  39.9 363.4 %all-reduce.6.cloned.1.call-start = ((), (), s32[]{:S(2)}) async-start(), calls=%async_computation.2 | async-start | bytes 4194304 | tf_op jit(solution)/shard_map/psum | solution.py:88
  63.7 11.9 %copy-start.4 = (s32[32]{0:T(128)S(1)}, s32[32]{0:T(128)}, u32[]{:S(2)}) copy-start(s32[32]{0:T(128)} %param.13) | copy-start | bytes 388
  168.5 3.1 copy-start.2
  262.2 14.3 %copy-start.3 = (bf16[512,512]{1,0:T(8,128)(2,1)S(1)}, bf16[512,512]{1,0:T(8,128)(2,1)}, u32[]{:S(2)}) copy-start(bf16[512,512]{1,0:T(8,128)(2,1)} %param.10) | copy-start | bytes 1572868
  276.4 142.1 %reduce-scatter.2.cloned.1.call-start = ((), (), s32[]{:S(2)}) async-start(), calls=%async_computation.3 | async-start | bytes 196608 | tf_op jit(solution)/shard_map/reduce_scatter | solution.py:106
  407.1 11.3 %copy-start.1 = (bf16[512,512]{1,0:T(8,128)(2,1)S(1)}, bf16[512,512]{1,0:T(8,128)(2,1)}, u32[]{:S(2)}) copy-start(bf16[512,512]{1,0:T(8,128)(2,1)} %param.9) | copy-start | bytes 1572868
Sparse Core Ops, SparseCore 0:
  40.0 128.4 all-reduce.7
  276.5 126.7 all-reduce.5
  411.6 6.8 reduce-scatter.1
